TPU v7x, 32 devices: a whole 2x2x4 slice. The times are simulated.
32 devices in a mesh: ctx: 4 (over y, x), head: 4 (over z), fsdp: 2 (over core).
Axes of the slice: x: 2, y: 2, z: 4, core: 2. Of those that a mesh axis runs over, the one named last changes fastest.
Arguments:
- layer_input: bfloat16 [4096, 4096], P(('ctx', 'fsdp')), may hold values from -6 to 6
- query_act: bfloat16 [4096, 4096], P(('ctx', 'fsdp'), 'head'), may hold values from -6 to 6
- key_act: bfloat16 [4096, 4096], P(('ctx', 'fsdp'), 'head'), may hold values from -6 to 6
- out_grad: bfloat16 [4096, 4096], P(('ctx', 'fsdp'), 'head'), may hold values from -6 to 6
- value_weight: bfloat16 [4096, 4096], P('fsdp', 'head'), may hold values from -0.09375 to 0.09375
Outputs:
- query_grad: bfloat16 [4096, 4096], P(('ctx', 'fsdp'), 'head')
- key_grad: bfloat16 [4096, 4096], P(('ctx', 'fsdp'), 'head')
- input_grad: bfloat16 [4096, 4096], P(('ctx', 'fsdp'), 'head')
- weight_grad: float32 [4096, 4096], P(('ctx', 'fsdp'), 'head')
All inputs are finite; a program needn't handle non-finite values.
Results may differ from a plain program's by a relative error of at most 0.018.
Values may be sent and summed in bfloat16 or wider, within the bound.
A program may use at most 128 MiB of HBM per device.

v0:
```python
import math
import jax
import jax.numpy as jnp
from jax import lax
from jax.sharding import PartitionSpec as P

HDIM = 128


def entering(array, axis, join, neutral):
    place = lax.axis_index(axis)
    gathered = lax.all_gather(array.astype(jnp.bfloat16), axis)
    state = jnp.zeros_like(array) + jnp.asarray(neutral, array.dtype)

    def one(step, state):
        return join(state, lax.dynamic_index_in_dim(gathered, step, 0, False).astype(array.dtype))

    return lax.fori_loop(0, place, one, state)


def as_sent(array):
    return jax.tree.map(lambda a: a.astype(jnp.bfloat16) if a.dtype == jnp.float32 else a, array)


def product(pattern, former, latter):
    return jnp.einsum(pattern, former, latter, precision=lax.Precision.HIGHEST)


def lowdot(pattern, former, latter):
    return jnp.einsum(pattern, former, latter, preferred_element_type=jnp.float32)


def add_states(earlier, following):
    return earlier + following


def norm_grad(attended, grad_heads):
    inverse_rms = lax.rsqrt(jnp.mean(attended * attended, axis=-1, keepdims=True) + 1e-05)
    normed = attended * inverse_rms
    return inverse_rms * (
        grad_heads - normed * jnp.mean(grad_heads * normed, axis=-1, keepdims=True)
    )


def local(layer_input, query_act, key_act, out_grad, value_weight):
    tok_rows = layer_input.shape[0]
    weight_full = lax.all_gather(value_weight, "fsdp", axis=0, tiled=True)
    value_act = jnp.dot(layer_input, weight_full, preferred_element_type=jnp.float32).astype(
        jnp.bfloat16
    )
    heads_dev = query_act.shape[1] // HDIM
    head_shape = (tok_rows, heads_dev, HDIM)
    query_heads = query_act.reshape(head_shape)
    key_heads = key_act.reshape(head_shape)
    value_heads = value_act.reshape(head_shape)
    query_wide = query_heads.astype(jnp.float32)
    key_wide = key_heads.astype(jnp.float32)
    value_wide = value_heads.astype(jnp.float32)
    grad_wide = out_grad.reshape(head_shape).astype(jnp.float32)
    pair_sum = lowdot("shi,shj->hij", key_heads, value_heads)
    state_prev = entering(pair_sum, ("ctx", "fsdp"), add_states, jnp.zeros_like(pair_sum))
    causal = jnp.tril(jnp.ones((tok_rows, tok_rows), dtype=bool))
    scores = lowdot("thi,shi->hts", query_heads, key_heads)
    masked = jnp.where(causal[None], scores, 0.0).astype(jnp.bfloat16)
    attended = lowdot("hts,shj->thj", masked, value_heads) + product(
        "thi,hij->thj", query_wide, state_prev
    )
    attn_grad = norm_grad(attended, grad_wide)
    attn_low = attn_grad.astype(jnp.bfloat16)
    local_grad = product("thi,thj->hij", query_wide, attn_grad)
    own_index = lax.axis_index(("ctx", "fsdp"))
    gathered = lax.all_gather(as_sent(local_grad[None]), ("ctx", "fsdp"), axis=0, tiled=True)
    owners = jnp.arange(gathered.shape[0], dtype=jnp.int32)
    is_later = (owners > own_index)[:, None, None, None]
    state_grad = jnp.zeros_like(local_grad) + jnp.sum(jnp.where(is_later, gathered, 0.0), axis=0)
    cross_terms = jnp.where(
        causal[None], lowdot("thj,shj->hts", attn_low, value_heads), 0.0
    ).astype(jnp.bfloat16)
    query_part = lowdot("hts,shi->thi", cross_terms, key_heads) + product(
        "hij,thj->thi", state_prev, attn_grad
    )
    key_part = lowdot("hts,thi->shi", cross_terms, query_heads) + product(
        "hij,shj->shi", state_grad, value_wide
    )
    value_part = lowdot("hts,thj->shj", masked, attn_low) + product(
        "shi,hij->shj", key_wide, state_grad
    )
    query_grad = query_part.reshape(tok_rows, -1).astype(jnp.bfloat16)
    key_grad = key_part.reshape(tok_rows, -1).astype(jnp.bfloat16)
    value_grad = value_part.reshape(tok_rows, -1).astype(jnp.bfloat16)
    seq_devices = lax.axis_size(("ctx", "fsdp"))
    grad_scale = 1.0 / math.sqrt(tok_rows * seq_devices)
    weight_grad = lax.psum_scatter(
        (
            lax.dot_general(
                layer_input,
                value_grad,
                (((0,), (0,)), ((), ())),
                preferred_element_type=jnp.float32,
            )
            * grad_scale
        ).astype(jnp.bfloat16),
        ("ctx", "fsdp"),
        scatter_dimension=0,
        tiled=True,
    ).astype(jnp.float32)
    partial_input = lax.dot_general(
        value_grad, weight_full, (((1,), (1,)), ((), ())), preferred_element_type=jnp.float32
    )
    input_grad = lax.psum_scatter(
        partial_input.astype(jnp.bfloat16), "head", scatter_dimension=1, tiled=True
    )
    return (query_grad, key_grad, input_grad, weight_grad)


def solution(mesh):
    in_specs = (
        P(("ctx", "fsdp"), None),
        P(("ctx", "fsdp"), "head"),
        P(("ctx", "fsdp"), "head"),
        P(("ctx", "fsdp"), "head"),
        P("fsdp", "head"),
    )
    out_specs = (
        P(("ctx", "fsdp"), "head"),
        P(("ctx", "fsdp"), "head"),
        P(("ctx", "fsdp"), "head"),
        P(("ctx", "fsdp"), "head"),
    )
    return jax.shard_map(local, mesh=mesh, in_specs=in_specs, out_specs=out_specs, check_vma=False)
```

profile of v0, /device:TPU:0, one launch (start us, length us, event | category | flops | bytes accessed | tf_op | source)
XLA Modules:
  0.0 283.1 jit_solution(3473864413043663214)
XLA Ops:
  8.0 24.2 %all-gather.6.cloned.1.call-done = bf16[4096,1024]{1,0:T(8,128)(2,1)} async-done(((bf16[2048,1024]{1,0:T(8,128)(2,1)}), bf16[4096,1024]{1,0:T(8,128)(2,1)}) %all-gather.6.cloned.1.call-update) | async-done | bytes 8388624 | tf_op jit(solution)/shard_map/all_gather | solution.py:47
  32.1 9.1 %fusion.2 = bf16[64,8,8,128]{3,2,1,0:T(8,128)(2,1)S(1)} fusion(bf16[512,4096]{1,0:T(8,128)(2,1)} %param.7, bf16[4096,1024]{1,0:T(8,128)(2,1)} %all-gather.6.cloned.1.call-done), kind=kOutput, calls=%fused_computation.17 | convolution fusion | flops 4295491584 | bytes 13631488 | tf_op jit(solution)/shard_map/dot_general | solution.py:48
  42.8 2.6 copy.60
  45.5 1.3 select_convert_fusion.1
  46.8 2.0 copy-done.5
  48.8 2.9 %fusion.16 = f32[8,128,512]{2,1,0:T(8,128)} fusion(bf16[8,512,512]{2,1,0:T(8,128)(2,1)S(1)} %select_convert_fusion.1, bf16[64,8,8,128]{3,2,1,0:T(8,128)(2,1)S(1)} %fusion.2), kind=kOutput, calls=%fused_computation.33 | convolution fusion | flops 536870912 | bytes 7340032 | tf_op jit(solution)/shard_map/hts,shj->thj/dot_general | solution.py:30
  51.6 20.2 %all-gather.8.cloned.1.call-done = bf16[64,128,128]{2,1,0:T(8,128)(2,1)} async-done(((bf16[8,128,128]{2,1,0:T(8,128)(2,1)}), bf16[64,128,128]{2,1,0:T(8,128)(2,1)}) %all-gather.8.cloned.1.call-update) | async-done | bytes 2097168 | tf_op jit(solution)/shard_map/all_gather | solution.py:12
  71.9 3.0 %fusion.1 = (f32[512,8]{0,1:T(8,128)S(1)}, f32[8,128,512]{2,1,0:T(8,128)S(1)}) fusion(f32[8,128,512]{2,1,0:T(8,128)} %fusion.16, f32[8,128,128]{2,1,0:T(8,128)S(1)} %get-tuple-element.27, bf16[512,1024]{1,0:T(8,128)(2,1)S(1)} %copy-done), kind=kOutput, calls=%fused_computation.8 | convolution fusion | flops 806875136 | bytes 5783552 | tf_op jit(solution)/shard_map/thi,hij->thj/dot_general | solution.py:26
  76.1 1.2 fusion.3
  78.4 4.2 %fusion.32 = f32[8,128,512]{2,1,0:T(8,128)} fusion(bf16[8,512,512]{2,1,0:T(8,128)(2,1)} %copy-done.5, f32[512,8,128]{0,2,1:T(8,128)S(1)} %subtract_multiply_fusion), kind=kOutput, calls=%fused_computation.50 | convolution fusion | flops 537395200 | bytes 8388608 | tf_op jit(solution)/shard_map/hts,thj->shj/dot_general | solution.py:30
  82.6 31.0 %all-gather.10.cloned.1.call-done = bf16[64,128,128]{2,1,0:T(8,128)(2,1)} async-done(((bf16[8,128,128]{2,1,0:T(8,128)(2,1)}), bf16[64,128,128]{2,1,0:T(8,128)(2,1)}) %all-gather.10.cloned.1.call-update) | async-done | bytes 2097168 | tf_op jit(solution)/shard_map/all_gather | solution.py:72
  113.6 2.2 select_reduce_fusion
  115.9 1.9 add_convert_fusion
  118.7 6.8 %fusion = bf16[4096,1024]{0,1:T(8,128)(2,1)} fusion(bf16[512,1024]{0,1:T(8,128)(2,1)S(1)} %bitcast.110, bf16[512,4096]{1,0:T(8,128)(2,1)S(1)} %copy-done.13), kind=kOutput, calls=%fused_computation.4 | convolution fusion | flops 4303355904 | bytes 13631488 | tf_op jit(solution)/shard_map/dot_general | solution.py:95
  125.6 10.6 %convolution_convert_fusion = bf16[512,4096]{1,0:T(8,128)(2,1)} fusion(bf16[512,1024]{0,1:T(8,128)(2,1)} %bitcast.111, bf16[4096,1024]{1,0:T(8,128)(2,1)} %all-gather.6.cloned.1.call-done), kind=kOutput, calls=%fused_computation.5 | convolution fusion | flops 4297064448 | bytes 13631488 | tf_op jit(solution)/shard_map/dot_general | solution.py:107
  136.2 3.0 %select_convert_fusion = bf16[8,512,512]{2,1,0:T(8,128)(2,1)S(1)} fusion(pred[512,512]{1,0:T(8,128)(4,1)} %copy-done.12, bf16[64,8,8,128]{3,2,1,0:T(8,128)(2,1)} %copy-done.6, f32[512,8,128]{0,2,1:T(8,128)S(1)} %subtract_multiply_fusion), kind=kOutput, calls=%fused_computation.2 | convolution fusion | flops 541589504 | bytes 7602176 | tf_op jit(solution)/shard_map/thj,shj->hts/dot_general | solution.py:30
  139.2 1.5 fusion.5
  141.2 3.0 %add_convert_fusion.2 = bf16[8,512,128]{1,2,0:T(8,128)(2,1)} fusion(f32[8,512,128]{1,2,0:T(8,128)S(1)} %fusion.5, f32[512,8,128]{0,2,1:T(8,128)S(1)} %subtract_multiply_fusion, f32[8,128,128]{2,1,0:T(8,128)S(1)} %copy-done.3), kind=kOutput, calls=%fused_computation.12 | convolution fusion | flops 806354944 | bytes 5767168 | tf_op jit(solution)/shard_map/hij,thj->thi/dot_general | solution.py:26
  144.3 2.3 copy.71
  146.5 3.1 %fusion.10 = f32[8,512,128]{1,2,0:T(8,128)S(1)} fusion(bf16[8,512,512]{2,1,0:T(8,128)(2,1)} %copy-done.1, bf16[512,1024]{1,0:T(8,128)(2,1)S(1)} %copy-done), kind=kOutput, calls=%fused_computation.27 | convolution fusion | flops 536870912 | bytes 7340032 | tf_op jit(solution)/shard_map/hts,thi->shi/dot_general | solution.py:30
  150.1 1.3 copy.72
  151.4 45.6 %reduce-scatter.5.cloned.1.call-done = bf16[512,1024]{0,1:T(8,128)(2,1)} async-done(((bf16[4096,1024]{0,1:T(8,128)(2,1)}), bf16[512,1024]{0,1:T(8,128)(2,1)}) %reduce-scatter.5.cloned.1.call-update) | async-done | bytes 1048592 | tf_op jit(solution)/shard_map/reduce_scatter | solution.py:93
  197.0 2.6 copy.73
  199.5 77.0 %reduce-scatter.3.cloned.1.call-done = bf16[512,1024]{1,0:T(8,128)(2,1)} async-done(((bf16[512,4096]{1,0:T(8,128)(2,1)}), bf16[512,1024]{1,0:T(8,128)(2,1)}) %reduce-scatter.3.cloned.1.call-update) | async-done | bytes 1048592 | tf_op jit(solution)/shard_map/reduce_scatter | solution.py:110
  (49 shorter events, 6.6 us)
Async XLA Ops:
  7.2 38.3 %copy-start = (bf16[512,1024]{1,0:T(8,128)(2,1)S(1)}, bf16[512,1024]{1,0:T(8,128)(2,1)}, u32[]{:S(2)}) copy-start(bf16[512,1024]{1,0:T(8,128)(2,1)} %param.8) | copy-start | bytes 3145732
  7.2 25.0 %all-gather.6.cloned.1.call-start = ((), (), s32[]{:S(2)}) async-start(), calls=%async_computation.2 | async-start | bytes 12582912 | tf_op jit(solution)/shard_map/all_gather | solution.py:47
  7.9 33.4 %copy-start.9 = (bf16[512,1024]{1,0:T(8,128)(2,1)S(1)}, bf16[512,1024]{1,0:T(8,128)(2,1)}, u32[]{:S(2)}) copy-start(bf16[512,1024]{1,0:T(8,128)(2,1)} %param.9) | copy-start | bytes 3145732
  7.9 63.9 %all-gather.8.cloned.1.call-start = ((), (), s32[]{:S(2)}) async-start(), calls=%async_computation.5 | async-start | bytes 2359296 | tf_op jit(solution)/shard_map/all_gather | solution.py:12
  41.3 5.5 %copy-start.6 = (bf16[64,8,8,128]{3,2,1,0:T(8,128)(2,1)}, bf16[64,8,8,128]{3,2,1,0:T(8,128)(2,1)S(1)}, u32[]{:S(2)}) copy-start(bf16[64,8,8,128]{3,2,1,0:T(8,128)(2,1)S(1)} %fusion.2) | copy-start | bytes 3145732
  42.7 70.9 %all-gather.10.cloned.1.call-start = ((), (), s32[]{:S(2)}) async-start(), calls=%async_computation.6 | async-start | bytes 2359296 | tf_op jit(solution)/shard_map/all_gather | solution.py:72
  45.5 1.3 copy-start.12
  46.8 2.0 copy-start.5
  71.9 3.0 %copy-start.2 = (f32[8,128,128]{2,1,0:T(8,128)}, f32[8,128,128]{2,1,0:T(8,128)S(1)}, u32[]{:S(2)}) copy-start(f32[8,128,128]{2,1,0:T(8,128)S(1)} %get-tuple-element.27) | copy-start | bytes 1572868
  71.9 3.1 %copy-start.4 = (f32[512,1024]{0,1:T(8,128)S(1)}, f32[512,1024]{0,1:T(8,128)}, u32[]{:S(2)}) copy-start(f32[512,1024]{0,1:T(8,128)} %copy.60) | copy-start | bytes 6291460
  78.2 118.8 %reduce-scatter.5.cloned.1.call-start = ((), (), s32[]{:S(2)}) async-start(), calls=%async_computation.4 | async-start | bytes 9437184 | tf_op jit(solution)/shard_map/reduce_scatter | solution.py:93
  113.6 2.2 copy-start.8
  115.8 2.9 %copy-start.13 = (bf16[512,4096]{1,0:T(8,128)(2,1)S(1)}, bf16[512,4096]{1,0:T(8,128)(2,1)}, u32[]{:S(2)}) copy-start(bf16[512,4096]{1,0:T(8,128)(2,1)} %param.7) | copy-start | bytes 12582916
  117.8 1.0 copy-start.11
  125.5 151.0 %reduce-scatter.3.cloned.1.call-start = ((), (), s32[]{:S(2)}) async-start(), calls=%async_computation.3 | async-start | bytes 5242880 | tf_op jit(solution)/shard_map/reduce_scatter | solution.py:110
  136.2 3.0 %copy-start.10 = (bf16[512,1024]{1,0:T(8,128)(2,1)S(1)}, bf16[512,1024]{1,0:T(8,128)(2,1)}, u32[]{:S(2)}) copy-start(bf16[512,1024]{1,0:T(8,128)(2,1)} %param.9) | copy-start | bytes 3145732
  139.2 2.0 copy-start.1
  139.2 2.0 copy-start.3
  146.5 3.1 %copy-start.7 = (bf16[64,8,8,128]{3,2,1,0:T(8,128)(2,1)S(1)}, bf16[64,8,8,128]{3,2,1,0:T(8,128)(2,1)}, u32[]{:S(2)}) copy-start(bf16[64,8,8,128]{3,2,1,0:T(8,128)(2,1)} %copy-done.6) | copy-start | bytes 3145732
Sparse Core Ops, SparseCore 0:
  9.5 22.5 all-gather.5
  42.9 28.9 all-gather.7
  78.3 35.2 all-gather.9
  125.6 71.2 reduce-scatter.4
  199.7 76.7 reduce-scatter.2
where the time goes:
time: 283 us
  waiting for transfers between devices  199 us (70%)
  matrix products  52.6 us (19%)
  between operations  14.1 us (5%)
  local copies, waits for them, and re-layouts  13.9 us (5%)
  other arithmetic  3.41 us (1%)
    reduce_scatter x1, waiting for transfers between devices, local(): lax.psum_scatter(partial_input.astype(jnp.bfloat16), 'head', scatter_dime...  77 us
    reduce_scatter x1, waiting for transfers between devices, local(): lax.psum_scatter((lax.dot_general(layer_input, value_grad, (((0,), (0,)),...  45.6 us
    all_gather x1, waiting for transfers between devices, local(): lax.all_gather(as_sent(local_grad[None]), ('ctx', 'fsdp'), axis=0, tiled=...  31 us
    all_gather x1, waiting for transfers between devices, local(): weight_full = lax.all_gather(value_weight, 'fsdp', axis=0, tiled=True)  24.2 us
    all_gather x1, waiting for transfers between devices, entering(): gathered = lax.all_gather(array.astype(jnp.bfloat16), axis)  20.2 us
    dot_general x7, matrix products, lowdot(): jnp.einsum(pattern, former, latter, preferred_element_type=jnp.float32)  16.5 us
    dot_general x1, matrix products, local(): lax.dot_general(value_grad, weight_full, (((1,), (1,)), ((), ())), prefer...  10.6 us
    unnamed x31, local copies, waits for them, and re-layouts  9.62 us
  transfers between devices with their start and end apart: 5, of which 5 were waited for; matrix products, arithmetic and copies ran while one was open for 14% of the time, Pallas kernels for 0%

commit v1 on v0

--- a/solution.py
+++ b/solution.py
@@ -44,7 +44,10 @@
 
 def local(layer_input, query_act, key_act, out_grad, value_weight):
     tok_rows = layer_input.shape[0]
-    weight_full = lax.all_gather(value_weight, "fsdp", axis=0, tiled=True)
+    known = lax.axis_size("fsdp")
+    main = jnp.stack([value_weight] * known)
+    later = lax.all_to_all(main, "fsdp", 0, 0)
+    weight_full = jnp.concatenate(later, axis=0)
     value_act = jnp.dot(layer_input, weight_full, preferred_element_type=jnp.float32).astype(
         jnp.bfloat16
     )

time: 283 us -> 275 us (0.972)
  waiting for transfers between devices: 199 us -> 176 us
  blocking collectives: 0 us -> 12.3 us
  other arithmetic: 3.41 us -> 10.9 us
  matrix products: 52.6 us -> 47.7 us
    all_gather x1 -> x0, waiting for transfers between devices: 24.2 us -> none  [local(): weight_full = lax.all_gather(value_weight, 'fsdp', axis=0, tiled=True)]
    all_to_all x0 -> x1, blocking collectives: none -> 12.3 us  [local(): later = lax.all_to_all(main, 'fsdp', 0, 0)]
    another operation x0 -> x1, other arithmetic: none -> 7.51 us  [local(): main = jnp.stack([value_weight] * known)]
    dot_general x1, matrix products: 9.14 us -> 4.54 us  [local(): jnp.dot(layer_input, weight_full, preferred_element_type=jnp.float32)]
    unnamed x31 -> x35, local copies, waits for them, and re-layouts: 9.62 us -> 9.56 us
  transfers between devices with their start and end apart: 5 -> 4, of which waited for: 5 -> 4; matrix products, arithmetic and copies ran while one was open for 14% -> 14% of each run, Pallas kernels for 0% -> 0%
where the time goes in v1:
time: 275 us
  waiting for transfers between devices  176 us (64%)
  matrix products  47.7 us (17%)
  between operations  14.1 us (5%)
  local copies, waits for them, and re-layouts  13.8 us (5%)
  blocking collectives  12.3 us (4%)
  other arithmetic  10.9 us (4%)
    reduce_scatter x1, waiting for transfers between devices, local(): lax.psum_scatter(partial_input.astype(jnp.bfloat16), 'head', scatter_dime...  77 us
    reduce_scatter x1, waiting for transfers between devices, local(): lax.psum_scatter((lax.dot_general(layer_input, value_grad, (((0,), (0,)),...  45.5 us
    all_gather x1, waiting for transfers between devices, local(): lax.all_gather(as_sent(local_grad[None]), ('ctx', 'fsdp'), axis=0, tiled=...  31.2 us
    all_gather x1, waiting for transfers between devices, entering(): gathered = lax.all_gather(array.astype(jnp.bfloat16), axis)  21.8 us
    dot_general x7, matrix products, lowdot(): jnp.einsum(pattern, former, latter, preferred_element_type=jnp.float32)  16.3 us
    all_to_all x1, blocking collectives, local(): later = lax.all_to_all(main, 'fsdp', 0, 0)  12.3 us
    dot_general x1, matrix products, local(): lax.dot_general(value_grad, weight_full, (((1,), (1,)), ((), ())), prefer...  10.6 us
    dot_general x5, matrix products, product(): return jnp.einsum(pattern, former, latter, precision=lax.Precision.HIGHEST)  9.56 us
  transfers between devices with their start and end apart: 4, of which 4 were waited for; matrix products, arithmetic and copies ran while one was open for 14% of the time, Pallas kernels for 0%

profile of v1, /device:TPU:0, one launch (start us, length us, event | category | flops | bytes accessed | tf_op | source)
XLA Modules:
  0.0 275.0 jit_solution(5808316055956517193)
XLA Ops:
  7.2 7.5 %pad_maximum_fusion = bf16[2,2048,1024]{2,1,0:T(8,128)(2,1)} fusion(bf16[1,2048,1024]{2,1,0:T(8,128)(2,1)} %bitcast.111), kind=kLoop, calls=%fused_computation.2 | loop fusion | flops 4194304 | bytes 12582912 | tf_op jit(solution)/shard_map/stack | solution.py:48
  14.7 12.3 %all_to_all.5 = bf16[2,2048,1024]{2,1,0:T(8,128)(2,1)S(1)} all-to-all(bf16[2,2048,1024]{2,1,0:T(8,128)(2,1)} %pad_maximum_fusion), channel_id=1, replica_groups=mesh['ctx'=4,'head'=4,'fsdp'=2] {'fsdp'}, dimensions={0} | all-to-all | bytes 16777216 | tf_op jit(solution)/shard_map/all_to_all | solution.py:49
  27.1 4.5 %convolution_convert_fusion.1 = bf16[1024,512]{1,0:T(8,128)(2,1)S(1)} fusion(bf16[4096,1024]{1,0:T(8,128)(2,1)S(1)} %bitcast.109, bf16[512,4096]{1,0:T(8,128)(2,1)S(1)} %copy-done.14), kind=kOutput, calls=%fused_computation.17 | convolution fusion | flops 4295491584 | bytes 13631488 | tf_op jit(solution)/shard_map/dot_general | solution.py:51
  33.1 2.6 copy.54
  35.7 1.3 select_convert_fusion.1
  37.1 2.0 copy-done.5
  39.0 2.8 %fusion.25 = f32[8,128,512]{2,1,0:T(8,128)} fusion(bf16[512,8,128]{0,2,1:T(8,128)(2,1)S(1)} %bitcast.106, bf16[8,512,512]{2,1,0:T(8,128)(2,1)S(1)} %select_convert_fusion.1), kind=kOutput, calls=%fused_computation.47 | convolution fusion | flops 536870912 | bytes 7340032 | tf_op jit(solution)/shard_map/hts,shj->thj/dot_general | solution.py:30
  41.8 21.8 %all-gather.5.cloned.1.call-done = bf16[64,128,128]{2,1,0:T(8,128)(2,1)} async-done(((bf16[8,128,128]{2,1,0:T(8,128)(2,1)}), bf16[64,128,128]{2,1,0:T(8,128)(2,1)}) %all-gather.5.cloned.1.call-update) | async-done | bytes 2097168 | tf_op jit(solution)/shard_map/all_gather | solution.py:12
  63.9 3.0 %fusion.1 = (f32[512,8]{0,1:T(8,128)S(1)}, f32[8,128,512]{2,1,0:T(8,128)S(1)}) fusion(f32[8,128,512]{2,1,0:T(8,128)} %fusion.25, f32[8,128,128]{2,1,0:T(8,128)S(1)} %get-tuple-element.27, bf16[512,1024]{1,0:T(8,128)(2,1)S(1)} %copy-done), kind=kOutput, calls=%fused_computation.9 | convolution fusion | flops 806875136 | bytes 5783552 | tf_op jit(solution)/shard_map/thi,hij->thj/dot_general | solution.py:26
  70.2 4.2 %fusion.22 = f32[8,128,512]{2,1,0:T(8,128)} fusion(bf16[8,512,512]{2,1,0:T(8,128)(2,1)} %copy-done.5, f32[512,8,128]{0,2,1:T(8,128)S(1)} %subtract_multiply_fusion), kind=kOutput, calls=%fused_computation.41 | convolution fusion | flops 537395200 | bytes 8388608 | tf_op jit(solution)/shard_map/hts,thj->shj/dot_general | solution.py:30
  74.4 31.2 %all-gather.7.cloned.1.call-done = bf16[64,128,128]{2,1,0:T(8,128)(2,1)} async-done(((bf16[8,128,128]{2,1,0:T(8,128)(2,1)}), bf16[64,128,128]{2,1,0:T(8,128)(2,1)}) %all-gather.7.cloned.1.call-update) | async-done | bytes 2097168 | tf_op jit(solution)/shard_map/all_gather | solution.py:75
  105.6 2.2 select_reduce_fusion
  107.9 1.9 add_convert_fusion
  110.7 6.7 %fusion = bf16[4096,1024]{0,1:T(8,128)(2,1)} fusion(bf16[512,1024]{0,1:T(8,128)(2,1)S(1)} %bitcast.115, bf16[512,4096]{1,0:T(8,128)(2,1)S(1)} %copy-done.15), kind=kOutput, calls=%fused_computation.5 | convolution fusion | flops 4303355904 | bytes 13631488 | tf_op jit(solution)/shard_map/dot_general | solution.py:98
  117.7 10.6 %convolution_convert_fusion = bf16[512,4096]{1,0:T(8,128)(2,1)} fusion(bf16[512,1024]{0,1:T(8,128)(2,1)} %bitcast.116, bf16[4096,1024]{1,0:T(8,128)(2,1)} %bitcast.110), kind=kOutput, calls=%fused_computation.6 | convolution fusion | flops 4297064448 | bytes 13631488 | tf_op jit(solution)/shard_map/dot_general | solution.py:110
  128.3 3.0 %select_convert_fusion = bf16[8,512,512]{2,1,0:T(8,128)(2,1)S(1)} fusion(pred[512,512]{1,0:T(8,128)(4,1)} %copy-done.13, bf16[512,8,128]{0,2,1:T(8,128)(2,1)} %bitcast.107, f32[512,8,128]{0,2,1:T(8,128)S(1)} %subtract_multiply_fusion), kind=kOutput, calls=%fused_computation.3 | convolution fusion | flops 541589504 | bytes 7602176 | tf_op jit(solution)/shard_map/thj,shj->hts/dot_general | solution.py:30
  131.3 1.5 fusion.4
  133.2 3.0 %add_convert_fusion.2 = bf16[8,512,128]{1,2,0:T(8,128)(2,1)} fusion(f32[8,512,128]{1,2,0:T(8,128)S(1)} %fusion.4, f32[512,8,128]{0,2,1:T(8,128)S(1)} %subtract_multiply_fusion, f32[8,128,128]{2,1,0:T(8,128)S(1)} %copy-done.3), kind=kOutput, calls=%fused_computation.13 | convolution fusion | flops 806354944 | bytes 5767168 | tf_op jit(solution)/shard_map/hij,thj->thi/dot_general | solution.py:26
  136.3 2.3 copy.65
  138.6 3.1 %fusion.9 = f32[8,512,128]{1,2,0:T(8,128)S(1)} fusion(bf16[8,512,512]{2,1,0:T(8,128)(2,1)} %copy-done.1, bf16[512,1024]{1,0:T(8,128)(2,1)S(1)} %copy-done), kind=kOutput, calls=%fused_computation.27 | convolution fusion | flops 536870912 | bytes 7340032 | tf_op jit(solution)/shard_map/hts,thi->shi/dot_general | solution.py:30
  142.1 1.3 copy.66
  143.4 45.5 %reduce-scatter.5.cloned.1.call-done = bf16[512,1024]{0,1:T(8,128)(2,1)} async-done(((bf16[4096,1024]{0,1:T(8,128)(2,1)}), bf16[512,1024]{0,1:T(8,128)(2,1)}) %reduce-scatter.5.cloned.1.call-update) | async-done | bytes 1048592 | tf_op jit(solution)/shard_map/reduce_scatter | solution.py:96
  188.9 2.6 copy.67
  191.5 77.0 %reduce-scatter.3.cloned.1.call-done = bf16[512,1024]{1,0:T(8,128)(2,1)} async-done(((bf16[512,4096]{1,0:T(8,128)(2,1)}), bf16[512,1024]{1,0:T(8,128)(2,1)}) %reduce-scatter.3.cloned.1.call-update) | async-done | bytes 1048592 | tf_op jit(solution)/shard_map/reduce_scatter | solution.py:113
  (52 shorter events, 7.1 us)
Async XLA Ops:
  7.2 28.5 %copy-start = (bf16[512,1024]{1,0:T(8,128)(2,1)S(1)}, bf16[512,1024]{1,0:T(8,128)(2,1)}, u32[]{:S(2)}) copy-start(bf16[512,1024]{1,0:T(8,128)(2,1)} %param.8) | copy-start | bytes 3145732
  7.2 56.5 %all-gather.5.cloned.1.call-start = ((), (), s32[]{:S(2)}) async-start(), calls=%async_computation.5 | async-start | bytes 2359296 | tf_op jit(solution)/shard_map/all_gather | solution.py:12
  14.7 12.3 %copy-start.14 = (bf16[512,4096]{1,0:T(8,128)(2,1)S(1)}, bf16[512,4096]{1,0:T(8,128)(2,1)}, u32[]{:S(2)}) copy-start(bf16[512,4096]{1,0:T(8,128)(2,1)} %param.7) | copy-start | bytes 12582916
  27.1 4.6 %copy-start.8 = (bf16[2,2048,1024]{2,1,0:T(8,128)(2,1)}, bf16[2,2048,1024]{2,1,0:T(8,128)(2,1)S(1)}, u32[]{:S(2)}) copy-start(bf16[2,2048,1024]{2,1,0:T(8,128)(2,1)S(1)} %all_to_all.5) | copy-start | bytes 25165828
  27.1 4.6 %copy-start.10 = (bf16[512,1024]{1,0:T(8,128)(2,1)S(1)}, bf16[512,1024]{1,0:T(8,128)(2,1)}, u32[]{:S(2)}) copy-start(bf16[512,1024]{1,0:T(8,128)(2,1)} %param.9) | copy-start | bytes 3145732
  31.6 5.4 %copy-start.6 = (bf16[1024,512]{1,0:T(8,128)(2,1)}, bf16[1024,512]{1,0:T(8,128)(2,1)S(1)}, u32[]{:S(2)}) copy-start(bf16[1024,512]{1,0:T(8,128)(2,1)S(1)} %convolution_convert_fusion.1) | copy-start | bytes 3145732
  33.0 72.6 %all-gather.7.cloned.1.call-start = ((), (), s32[]{:S(2)}) async-start(), calls=%async_computation.6 | async-start | bytes 2359296 | tf_op jit(solution)/shard_map/all_gather | solution.py:75
  35.7 1.3 copy-start.13
  37.1 2.0 copy-start.5
  63.9 3.0 %copy-start.2 = (f32[8,128,128]{2,1,0:T(8,128)}, f32[8,128,128]{2,1,0:T(8,128)S(1)}, u32[]{:S(2)}) copy-start(f32[8,128,128]{2,1,0:T(8,128)S(1)} %get-tuple-element.27) | copy-start | bytes 1572868
  63.9 3.1 %copy-start.4 = (f32[512,1024]{0,1:T(8,128)S(1)}, f32[512,1024]{0,1:T(8,128)}, u32[]{:S(2)}) copy-start(f32[512,1024]{0,1:T(8,128)} %copy.54) | copy-start | bytes 6291460
  70.1 118.8 %reduce-scatter.5.cloned.1.call-start = ((), (), s32[]{:S(2)}) async-start(), calls=%async_computation.4 | async-start | bytes 9437184 | tf_op jit(solution)/shard_map/reduce_scatter | solution.py:96
  105.6 2.2 copy-start.9
  107.8 2.9 %copy-start.15 = (bf16[512,4096]{1,0:T(8,128)(2,1)S(1)}, bf16[512,4096]{1,0:T(8,128)(2,1)}, u32[]{:S(2)}) copy-start(bf16[512,4096]{1,0:T(8,128)(2,1)} %param.7) | copy-start | bytes 12582916
  109.8 1.0 copy-start.12
  117.4 151.0 %reduce-scatter.3.cloned.1.call-start = ((), (), s32[]{:S(2)}) async-start(), calls=%async_computation.3 | async-start | bytes 5242880 | tf_op jit(solution)/shard_map/reduce_scatter | solution.py:113
  128.3 3.0 %copy-start.11 = (bf16[512,1024]{1,0:T(8,128)(2,1)S(1)}, bf16[512,1024]{1,0:T(8,128)(2,1)}, u32[]{:S(2)}) copy-start(bf16[512,1024]{1,0:T(8,128)(2,1)} %param.9) | copy-start | bytes 3145732
  131.3 2.0 copy-start.1
  131.3 1.9 copy-start.3
  138.6 3.1 %copy-start.7 = (bf16[1024,512]{1,0:T(8,128)(2,1)S(1)}, bf16[1024,512]{1,0:T(8,128)(2,1)}, u32[]{:S(2)}) copy-start(bf16[1024,512]{1,0:T(8,128)(2,1)} %copy-done.6) | copy-start | bytes 3145732
Sparse Core Ops, SparseCore 0:
  33.1 30.4 all-gather.4
  70.3 35.2 all-gather.6
  117.6 71.3 reduce-scatter.4
  191.6 76.7 reduce-scatter.2
